TPU v7x, 32 devices: a whole 2x2x4 slice. The times are simulated.
32 devices in a mesh: shot: 8 (over y, x, core), rcv: 4 (over z).
Axes of the slice: x: 2, y: 2, z: 4, core: 2. Of those that a mesh axis runs over, the one named last changes fastest.
Arguments:
- spectra: bfloat16 [4, 2, 2048, 2048], P(None, None, 'shot', 'rcv'), may hold values from -6 to 6
Outputs:
- multiples: float32 [4, 2, 2048, 2048], P('rcv', None, 'shot')
All inputs are finite; a program needn't handle non-finite values.
Results may differ from a plain program's by a relative error of at most 0.0003.
Values may be sent and summed in bfloat16 or wider, within the bound.
A program may use at most 128 MiB of HBM per device.

v0:
```python
import math
import jax
import jax.numpy as jnp
from jax import lax
from jax.sharding import PartitionSpec as P


def per_device(spectra):
    own_rows = lax.all_to_all(spectra, "rcv", split_axis=0, concat_axis=3, tiled=True)
    receiver_set_full = own_rows.shape[3]
    real_left_gathered = own_rows[:, 0]
    imaginary_left_gathered = own_rows[:, 1]
    shard_part = lax.all_gather(own_rows, "shot", axis=2, tiled=True)
    real_right_factor = shard_part[:, 0]
    imaginary_right_factor = shard_part[:, 1]
    real_out = jnp.einsum(
        "ang,agv->anv", real_left_gathered, real_right_factor, preferred_element_type=jnp.float32
    ) - jnp.einsum(
        "ang,agv->anv",
        imaginary_left_gathered,
        imaginary_right_factor,
        preferred_element_type=jnp.float32,
    )
    imag_out = jnp.einsum(
        "ang,agv->anv",
        real_left_gathered,
        imaginary_right_factor,
        preferred_element_type=jnp.float32,
    ) + jnp.einsum(
        "ang,agv->anv",
        imaginary_left_gathered,
        real_right_factor,
        preferred_element_type=jnp.float32,
    )
    result = jnp.stack([real_out, imag_out], axis=1)
    return result * (-1.0 / math.sqrt(receiver_set_full))


def solution(mesh):
    return jax.shard_map(
        per_device,
        mesh=mesh,
        in_specs=(P(None, None, "shot", "rcv"),),
        out_specs=P("rcv", None, "shot", None),
        check_vma=False,
    )
```

profile of v0, /device:TPU:0, one launch (start us, length us, event | category | flops | bytes accessed | tf_op | source)
XLA Modules:
  0.0 186.5 jit_solution(3624461053671120266)
XLA Ops:
  6.5 0.0 all-gather.2.cloned.1.call-start
  6.5 2.8 %copy.3 = bf16[4,2,256,512]{2,3,1,0:T(8,128)(2,1)S(1)} copy(bf16[4,2,256,512]{3,2,1,0:T(8,128)(2,1)} %param.1) | data formatting | bytes 4194304 | tf_op args[0]
  9.3 54.3 %all_to_all.18 = bf16[4,2,256,512]{2,3,1,0:T(8,128)(2,1)S(1)} all-to-all(bf16[4,2,256,512]{2,3,1,0:T(8,128)(2,1)S(1)} %copy.3), channel_id=1, replica_groups=mesh['shot'=8,'rcv'=4] {'rcv'}, dimensions={0} | all-to-all | bytes 4194304 | tf_op jit(solution)/shard_map/all_to_all | solution.py:9
  63.6 1.5 copy.4
  65.1 0.0 copy-start
  65.1 0.0 all-gather.2.cloned.1.call-update
  65.1 92.5 %all-gather.2.cloned.1.call-done = bf16[1,2,2048,2048]{2,3,1,0:T(8,128)(2,1)} async-done(((bf16[1,2,256,2048]{2,3,1,0:T(8,128)(2,1)}), bf16[1,2,2048,2048]{2,3,1,0:T(8,128)(2,1)}) %all-gather.2.cloned.1.call-update) | async-done | bytes 16777232 | tf_op jit(solution)/shard_map/all_gather | solution.py:13
  157.6 0.0 copy-done
  157.6 0.0 slice-start
  157.6 0.0 slice-start.1
  157.6 0.0 slice-start.2
  157.6 5.9 %fusion = f32[256,2048]{1,0:T(8,128)S(1)} fusion(bf16[1,2,2048,2048]{2,3,1,0:T(8,128)(2,1)} %all-gather.2.cloned.1.call-done, bf16[1,2,256,2048]{2,3,1,0:T(8,128)(2,1)S(1)} %bitcast.34), kind=kOutput, calls=%fused_computation.2 | convolution fusion | flops 2147483648 | bytes 11534336 | tf_op jit(solution)/shard_map/ang,agv->anv/dot_general | solution.py:29
  163.5 0.0 slice-start.3
  163.5 7.2 %fusion.1 = f32[256,2048]{1,0:T(8,128)} fusion(bf16[1,2,2048,2048]{2,3,1,0:T(8,128)(2,1)} %all-gather.2.cloned.1.call-done, bf16[1,2,256,2048]{2,3,1,0:T(8,128)(2,1)S(1)} %bitcast.35), kind=kOutput, calls=%fused_computation.3 | convolution fusion | flops 2147483648 | bytes 11534336 | tf_op jit(solution)/shard_map/ang,agv->anv/dot_general | solution.py:16
  170.8 0.0 slice-done
  170.8 0.0 slice-done.1
  170.8 0.0 slice-done.2
  170.8 0.0 slice-done.3
  170.8 2.4 %fusion.7 = f32[1,1,256,2048]{3,2,1,0:T(8,128)S(1)} fusion(f32[256,2048]{1,0:T(8,128)S(1)} %fusion, bf16[1,2,2048,2048]{2,3,1,0:T(8,128)(2,1)S(1)} %bitcast.39, bf16[1,2,256,2048]{2,3,1,0:T(8,128)(2,1)S(1)} %bitcast.36), kind=kOutput, calls=%fused_computation.10 | convolution fusion | flops 2148007936 | bytes 13631488 | tf_op jit(solution)/shard_map/ang,agv->anv/dot_general | solution.py:24
  173.2 4.0 %fusion.5 = f32[1,1,256,2048]{3,2,1,0:T(8,128)S(1)} fusion(f32[256,2048]{1,0:T(8,128)} %fusion.1, bf16[1,2,2048,2048]{2,3,1,0:T(8,128)(2,1)S(1)} %bitcast.39, bf16[1,2,256,2048]{2,3,1,0:T(8,128)(2,1)S(1)} %bitcast.37), kind=kOutput, calls=%fused_computation.8 | convolution fusion | flops 2148007936 | bytes 13631488 | tf_op jit(solution)/shard_map/ang,agv->anv/dot_general | solution.py:18
  177.2 2.4 %maximum_multiply_fusion = f32[1,2,256,2048]{3,2,1,0:T(8,128)} fusion(f32[1,1,256,2048]{3,2,1,0:T(8,128)S(1)} %fusion.7, f32[1,1,256,2048]{3,2,1,0:T(8,128)S(1)} %fusion.5), kind=kLoop, calls=%fused_computation.6 | loop fusion | flops 2097152 | bytes 8388608 | tf_op jit(solution)/shard_map/mul | solution.py:36
  (1 shorter events, 0.0 us)
Async XLA Ops:
  6.5 151.1 %all-gather.2.cloned.1.call-start = ((), (), s32[]{:S(2)}) async-start(), calls=%async_computation.1 | async-start | bytes 18874368 | tf_op jit(solution)/shard_map/all_gather | solution.py:13
  65.1 92.5 %copy-start = (bf16[4,2,256,512]{2,3,0,1:T(8,128)(2,1)S(1)}, bf16[4,2,256,512]{2,3,0,1:T(8,128)(2,1)}, u32[]{:S(2)}) copy-start(bf16[4,2,256,512]{2,3,0,1:T(8,128)(2,1)} %copy.4) | copy-start | bytes 6291460
  157.6 13.2 %slice-start = ((s8[16777216]{0:T(1024)(128)(4,1)}), s8[4194304]{0:T(1024)(128)(4,1)S(1)}, s32[]{:S(2)}) async-start(s8[16777216]{0:T(1024)(128)(4,1)} %bitcast.38), calls=%async_computation.2 | async-start | bytes 8388608
  157.6 13.2 %slice-start.1 = ((s8[16777216]{0:T(1024)(128)(4,1)}), s8[4194304]{0:T(1024)(128)(4,1)S(1)}, s32[]{:S(2)}) async-start(s8[16777216]{0:T(1024)(128)(4,1)} %bitcast.38), calls=%async_computation.3 | async-start | bytes 8388608
  157.6 13.2 %slice-start.2 = ((s8[16777216]{0:T(1024)(128)(4,1)}), s8[4194304]{0:T(1024)(128)(4,1)S(1)}, s32[]{:S(2)}) async-start(s8[16777216]{0:T(1024)(128)(4,1)} %bitcast.38), calls=%async_computation.4 | async-start | bytes 8388608
  163.5 7.3 %slice-start.3 = ((s8[16777216]{0:T(1024)(128)(4,1)}), s8[4194304]{0:T(1024)(128)(4,1)S(1)}, s32[]{:S(2)}) async-start(s8[16777216]{0:T(1024)(128)(4,1)} %bitcast.38), calls=%async_computation.5 | async-start | bytes 8388608
Sparse Core Ops, SparseCore 0:
  65.2 92.3 all-gather.1
where the time goes:
time: 187 us; the launch traced here: 186 us
  waiting for transfers between devices  92.5 us (49%)
  blocking collectives  54.3 us (29%)
  matrix products  19.5 us (10%)
  between operations  13.5 us (7%)
  local copies, waits for them, and re-layouts  4.23 us (2%)
  other arithmetic  2.43 us (1%)
    all_gather x1, waiting for transfers between devices, per_device(): shard_part = lax.all_gather(own_rows, 'shot', axis=2, tiled=True)  92.5 us
    all_to_all x1, blocking collectives, per_device(): lax.all_to_all(spectra, 'rcv', split_axis=0, concat_axis=3, tiled=True)  54.3 us
    dot_general x1, matrix products, per_device(): jnp.einsum('ang,agv->anv', real_left_gathered, real_right_factor, preferr...  7.24 us
    dot_general x1, matrix products, per_device(): jnp.einsum('ang,agv->anv', imaginary_left_gathered, real_right_factor, pr...  5.92 us
    dot_general x1, matrix products, per_device(): jnp.einsum('ang,agv->anv', imaginary_left_gathered, imaginary_right_facto...  3.98 us
  transfers between devices with their start and end apart: 1, of which 1 were waited for; matrix products, arithmetic and copies ran while one was open for 0% of the time, Pallas kernels for 0%

commit v1 on v0

--- a/solution.py
+++ b/solution.py
@@ -6,11 +6,34 @@
 
 
 def per_device(spectra):
+
+    def match_zones(s0, along_axis):
+        left_arr = lax.axis_index(along_axis)
+        r2 = lax.axis_size(along_axis)
+        placed, z1, v1 = (r2, left_arr, s0.shape[2])
+        q_next = tuple((s * placed if rr == 2 else s for rr, s in enumerate(s0.shape)))
+        inter = jnp.zeros(q_next, s0.dtype)
+        mixed_arr = lax.dynamic_update_slice_in_dim(inter, s0, z1 * v1, axis=2)
+        formed = w_next = s0
+        for u in range(1, placed // 2 + 1):
+            ready = tuple(((rr, (rr + 1) % placed) for rr in range(placed)))
+            formed = lax.ppermute(formed, along_axis, ready)
+            mixed_arr = lax.dynamic_update_slice_in_dim(
+                mixed_arr, formed, (z1 - u) % placed * v1, axis=2
+            )
+            if 2 * u < placed:
+                e_now = tuple(((rr, (rr - 1) % placed) for rr in range(placed)))
+                w_next = lax.ppermute(w_next, along_axis, e_now)
+                mixed_arr = lax.dynamic_update_slice_in_dim(
+                    mixed_arr, w_next, (z1 + u) % placed * v1, axis=2
+                )
+        return mixed_arr
+
     own_rows = lax.all_to_all(spectra, "rcv", split_axis=0, concat_axis=3, tiled=True)
     receiver_set_full = own_rows.shape[3]
     real_left_gathered = own_rows[:, 0]
     imaginary_left_gathered = own_rows[:, 1]
-    shard_part = lax.all_gather(own_rows, "shot", axis=2, tiled=True)
+    shard_part = match_zones(own_rows, "shot")
     real_right_factor = shard_part[:, 0]
     imaginary_right_factor = shard_part[:, 1]
     real_out = jnp.einsum(

time: 187 us -> 248 us (1.33)
  waiting for transfers between devices: 92.5 us -> 149 us
  local copies, waits for them, and re-layouts: 4.23 us -> 24.4 us
  between operations: 13.5 us -> 0.17 us
  matrix products: 19.5 us -> 10 us
  starting transfers between devices: 0.01 us -> 5.49 us
    ppermute x0 -> x7, waiting for transfers between devices: none -> 149 us  [the longest x4 149 us: match_zones(): formed = lax.ppermute(formed, along_axis, ready)]
    all_gather x1 -> x0, waiting for transfers between devices: 92.5 us -> none  [per_device(): shard_part = lax.all_gather(own_rows, 'shot', axis=2, tiled=True)]
    dynamic_update_slice x0 -> x8, local copies, waits for them, and re-layouts: none -> 9.23 us  [the longest x4 4.61 us: match_zones(): lax.dynamic_update_slice_in_dim(mixed_arr, formed, (z1 - u) % placed * v1...]
    ppermute x0 -> x7, starting transfers between devices: none -> 5.49 us  [the longest x3 5.43 us: match_zones(): w_next = lax.ppermute(w_next, along_axis, e_now)]
    mul x0 -> x1, local copies, waits for them, and re-layouts: none -> 5.34 us  [per_device(): return result * (-1.0 / math.sqrt(receiver_set_full))]
    unnamed x11 -> x13, local copies, waits for them, and re-layouts: 2.78 us -> 7.65 us
    dot_general x1, matrix products: 7.24 us -> 2.52 us  [per_device(): jnp.einsum('ang,agv->anv', real_left_gathered, real_right_factor, preferr...]
    dot_general x1, matrix products: 5.92 us -> 2.48 us  [per_device(): jnp.einsum('ang,agv->anv', imaginary_left_gathered, real_right_factor, pr...]
  transfers between devices with their start and end apart: 1 -> 7, of which waited for: 1 -> 4; matrix products, arithmetic and copies ran while one was open for 0% -> 4% of each run, Pallas kernels for 0% -> 0%
where the time goes in v1:
time: 248 us; the launch traced here: 246 us
  waiting for transfers between devices  149 us (60%)
  blocking collectives  54.3 us (22%)
  local copies, waits for them, and re-layouts  24.4 us (10%)
  matrix products  10 us (4%)
  starting transfers between devices  5.49 us (2%)
    ppermute x4, waiting for transfers between devices, match_zones(): formed = lax.ppermute(formed, along_axis, ready)  149 us
    all_to_all x1, blocking collectives, per_device(): lax.all_to_all(spectra, 'rcv', split_axis=0, concat_axis=3, tiled=True)  54.3 us
    unnamed x13, local copies, waits for them, and re-layouts  7.65 us
    ppermute x3, starting transfers between devices, match_zones(): w_next = lax.ppermute(w_next, along_axis, e_now)  5.43 us
    mul x1, local copies, waits for them, and re-layouts, per_device(): return result * (-1.0 / math.sqrt(receiver_set_full))  5.34 us
  transfers between devices with their start and end apart: 7, of which 4 were waited for; matrix products, arithmetic and copies ran while one was open for 4% of the time, Pallas kernels for 0%

profile of v1, /device:TPU:0, one launch (start us, length us, event | category | flops | bytes accessed | tf_op | source)
XLA Modules:
  0.0 246.0 jit_solution(545011859363614596)
XLA Ops:
  0.0 2.8 %copy.5 = bf16[4,2,256,512]{2,3,1,0:T(8,128)(2,1)S(1)} copy(bf16[4,2,256,512]{3,2,1,0:T(8,128)(2,1)} %param.1) | data formatting | bytes 4194304 | tf_op args[0]
  2.8 54.3 %all_to_all.18 = bf16[4,2,256,512]{2,3,1,0:T(8,128)(2,1)S(1)} all-to-all(bf16[4,2,256,512]{2,3,1,0:T(8,128)(2,1)S(1)} %copy.5), channel_id=1, replica_groups=mesh['shot'=8,'rcv'=4] {'rcv'}, dimensions={0} | all-to-all | bytes 4194304 | tf_op jit(solution)/shard_map/all_to_all | solution.py:32
  57.3 2.6 %collective-permute-start.1 = (bf16[1,2,256,2048]{2,3,1,0:T(8,128)(2,1)S(1)}, bf16[1,2,256,2048]{2,3,1,0:T(8,128)(2,1)S(1)}, u32[]{:S(2)}, u32[]{:S(2)}) collective-permute-start(bf16[1,2,256,2048]{2,3,1,0:T(8,128)(2,1)S(1)} %bitcast.38), channel_id=1, source_target_pairs={{0,28},{4,0},{8,4},{12,8},{16,12},{20,16},{24,20},{28,24},{1,29},{... | collective-permute-start | bytes 6291464 | tf_op jit(solution)/shard_map/ppermute | solution.py:26
  59.9 44.3 %collective-permute-done = bf16[1,2,256,2048]{2,3,1,0:T(8,128)(2,1)S(1)} collective-permute-done((bf16[1,2,256,2048]{2,3,1,0:T(8,128)(2,1)S(1)}, bf16[1,2,256,2048]{2,3,1,0:T(8,128)(2,1)S(1)}, u32[]{:S(2)}, u32[]{:S(2)}) %collective-permute-start) | collective-permute-done | bytes 2097184 | tf_op jit(solution)/shard_map/ppermute | solution.py:20
  104.2 1.3 copy-done
  105.5 1.5 collective-permute-start.3
  107.0 44.7 %collective-permute-done.2 = bf16[1,2,256,2048]{2,3,1,0:T(8,128)(2,1)S(1)} collective-permute-done((bf16[1,2,256,2048]{2,3,1,0:T(8,128)(2,1)S(1)}, bf16[1,2,256,2048]{2,3,1,0:T(8,128)(2,1)S(1)}, u32[]{:S(2)}, u32[]{:S(2)}) %collective-permute-start.2) | collective-permute-done | bytes 2097184 | tf_op jit(solution)/shard_map/ppermute | solution.py:20
  151.7 1.3 copy-done.4
  153.0 1.3 collective-permute-start.5
  154.3 45.3 %collective-permute-done.4 = bf16[1,2,256,2048]{2,3,1,0:T(8,128)(2,1)} collective-permute-done((bf16[1,2,256,2048]{2,3,1,0:T(8,128)(2,1)S(1)}, bf16[1,2,256,2048]{2,3,1,0:T(8,128)(2,1)}, u32[]{:S(2)}, u32[]{:S(2)}) %collective-permute-start.4) | collective-permute-done | bytes 2097184 | tf_op jit(solution)/shard_map/ppermute | solution.py:20
  199.7 2.0 broadcast_in_dim.3
  202.1 1.2 copy-done.1
  204.3 0.8 copy-done.5
  205.4 2.0 constant_dynamic-update-slice_fusion.3
  207.4 1.9 constant_dynamic-update-slice_fusion.2
  209.4 2.0 constant_dynamic-update-slice_fusion.1
  211.3 15.0 %collective-permute-done.6 = bf16[1,2,256,2048]{2,3,1,0:T(8,128)(2,1)} collective-permute-done((bf16[1,2,256,2048]{2,3,1,0:T(8,128)(2,1)}, bf16[1,2,256,2048]{2,3,1,0:T(8,128)(2,1)}, u32[]{:S(2)}, u32[]{:S(2)}) %collective-permute-start.6) | collective-permute-done | bytes 2097184 | tf_op jit(solution)/shard_map/ppermute | solution.py:20
  226.3 1.9 constant_dynamic-update-slice_fusion
  228.3 2.5 %fusion.3 = f32[2048,256]{1,0:T(8,128)S(1)} fusion(bf16[1,2,2048,2048]{2,3,1,0:T(8,128)(2,1)S(1)} %constant_dynamic-update-slice_fusion, bf16[1,2,256,2048]{2,3,1,0:T(8,128)(2,1)S(1)} %bitcast.40), kind=kOutput, calls=%fused_computation.5 | convolution fusion | flops 2147483648 | bytes 11534336 | tf_op jit(solution)/shard_map/ang,agv->anv/dot_general | solution.py:41
  230.8 2.5 %fusion = f32[2048,256]{1,0:T(8,128)S(1)} fusion(bf16[1,2,2048,2048]{2,3,1,0:T(8,128)(2,1)S(1)} %constant_dynamic-update-slice_fusion, bf16[1,2,256,2048]{2,3,1,0:T(8,128)(2,1)S(1)} %bitcast.41), kind=kOutput, calls=%fused_computation.2 | convolution fusion | flops 2147483648 | bytes 11534336 | tf_op jit(solution)/shard_map/ang,agv->anv/dot_general | solution.py:52
  233.3 2.5 %fusion.7 = f32[1,1,256,2048]{2,3,1,0:T(8,128)S(1)} fusion(f32[2048,256]{1,0:T(8,128)S(1)} %fusion.3, bf16[1,2,2048,2048]{2,3,1,0:T(8,128)(2,1)S(1)} %constant_dynamic-update-slice_fusion, bf16[1,2,256,2048]{2,3,1,0:T(8,128)(2,1)S(1)} %bitcast.42), kind=kOutput, calls=%fused_computation.10 | convolution fusion | flops 2148007936 | bytes 13631488 | tf_op jit(solution)/shard_map/ang,agv->anv/dot_general | solution.py:39
  235.8 2.5 %fusion.5 = f32[1,1,256,2048]{2,3,1,0:T(8,128)S(1)} fusion(f32[2048,256]{1,0:T(8,128)S(1)} %fusion, bf16[1,2,2048,2048]{2,3,1,0:T(8,128)(2,1)S(1)} %constant_dynamic-update-slice_fusion, bf16[1,2,256,2048]{2,3,1,0:T(8,128)(2,1)S(1)} %bitcast.43), kind=kOutput, calls=%fused_computation.8 | convolution fusion | flops 2148007936 | bytes 13631488 | tf_op jit(solution)/shard_map/ang,agv->anv/dot_general | solution.py:47
  238.3 2.3 maximum_multiply_fusion
  240.7 5.3 %copy.7 = f32[1,2,256,2048]{3,2,1,0:T(8,128)} copy(f32[1,2,256,2048]{2,3,1,0:T(8,128)} %maximum_multiply_fusion) | data formatting | bytes 8388608 | tf_op jit(solution)/shard_map/mul | solution.py:59
  (20 shorter events, 1.9 us)
Async XLA Ops:
  57.2 47.0 %collective-permute-start = (bf16[1,2,256,2048]{2,3,1,0:T(8,128)(2,1)S(1)}, bf16[1,2,256,2048]{2,3,1,0:T(8,128)(2,1)S(1)}, u32[]{:S(2)}, u32[]{:S(2)}) collective-permute-start(bf16[1,2,256,2048]{2,3,1,0:T(8,128)(2,1)S(1)} %bitcast.37), channel_id=1, source_target_pairs={{0,4},{4,8},{8,12},{12,16},{16,20},{20,24},{24,28},{28,0},{1,5},{5... | collective-permute-start | bytes 6291464 | tf_op jit(solution)/shard_map/ppermute | solution.py:20
  57.3 46.9 %collective-permute-start.1 = (bf16[1,2,256,2048]{2,3,1,0:T(8,128)(2,1)S(1)}, bf16[1,2,256,2048]{2,3,1,0:T(8,128)(2,1)S(1)}, u32[]{:S(2)}, u32[]{:S(2)}) collective-permute-start(bf16[1,2,256,2048]{2,3,1,0:T(8,128)(2,1)S(1)} %bitcast.38), channel_id=1, source_target_pairs={{0,28},{4,0},{8,4},{12,8},{16,12},{20,16},{24,20},{28,24},{1,29},{... | collective-permute-start | bytes 6291464 | tf_op jit(solution)/shard_map/ppermute | solution.py:26
  104.2 1.3 copy-start
  104.2 47.5 %collective-permute-start.2 = (bf16[1,2,256,2048]{2,3,1,0:T(8,128)(2,1)S(1)}, bf16[1,2,256,2048]{2,3,1,0:T(8,128)(2,1)S(1)}, u32[]{:S(2)}, u32[]{:S(2)}) collective-permute-start(bf16[1,2,256,2048]{2,3,1,0:T(8,128)(2,1)S(1)} %collective-permute-done), channel_id=1, source_target_pairs={{0,4},{4,8},{8,12},{12,16},{16,20},{20,24},{24,28},{28,0},{1,5},{5... | collective-permute-start | bytes 6291464 | tf_op jit(solution)/shard_map/ppermute | solution.py:20
  105.5 46.2 %copy-start.2 = (bf16[1,2,256,2048]{2,3,1,0:T(8,128)(2,1)}, bf16[1,2,256,2048]{2,3,1,0:T(8,128)(2,1)S(1)}, u32[]{:S(2)}) copy-start(bf16[1,2,256,2048]{2,3,1,0:T(8,128)(2,1)S(1)} %collective-permute-done.1) | copy-start | bytes 6291460
  105.5 46.2 %collective-permute-start.3 = (bf16[1,2,256,2048]{2,3,1,0:T(8,128)(2,1)S(1)}, bf16[1,2,256,2048]{2,3,1,0:T(8,128)(2,1)}, u32[]{:S(2)}, u32[]{:S(2)}) collective-permute-start(bf16[1,2,256,2048]{2,3,1,0:T(8,128)(2,1)S(1)} %collective-permute-done.1), channel_id=1, source_target_pairs={{0,28},{4,0},{8,4},{12,8},{16,12},{20,16},{24,20},{28,24},{1,29},{... | collective-permute-start | bytes 6291464 | tf_op jit(solution)/shard_map/ppermute | solution.py:26
  151.7 1.4 copy-start.4
  151.7 48.0 %collective-permute-start.4 = (bf16[1,2,256,2048]{2,3,1,0:T(8,128)(2,1)S(1)}, bf16[1,2,256,2048]{2,3,1,0:T(8,128)(2,1)}, u32[]{:S(2)}, u32[]{:S(2)}) collective-permute-start(bf16[1,2,256,2048]{2,3,1,0:T(8,128)(2,1)S(1)} %collective-permute-done.2), channel_id=1, source_target_pairs={{0,4},{4,8},{8,12},{12,16},{16,20},{20,24},{24,28},{28,0},{1,5},{5... | collective-permute-start | bytes 6291464 | tf_op jit(solution)/shard_map/ppermute | solution.py:20
  153.0 56.3 %collective-permute-start.5 = (bf16[1,2,256,2048]{2,3,1,0:T(8,128)(2,1)}, bf16[1,2,256,2048]{2,3,1,0:T(8,128)(2,1)}, u32[]{:S(2)}, u32[]{:S(2)}) collective-permute-start(bf16[1,2,256,2048]{2,3,1,0:T(8,128)(2,1)} %collective-permute-done.3), channel_id=1, source_target_pairs={{0,28},{4,0},{8,4},{12,8},{16,12},{20,16},{24,20},{28,24},{1,29},{... | collective-permute-start | bytes 6291464 | tf_op jit(solution)/shard_map/ppermute | solution.py:26
  199.7 26.7 %collective-permute-start.6 = (bf16[1,2,256,2048]{2,3,1,0:T(8,128)(2,1)}, bf16[1,2,256,2048]{2,3,1,0:T(8,128)(2,1)}, u32[]{:S(2)}, u32[]{:S(2)}) collective-permute-start(bf16[1,2,256,2048]{2,3,1,0:T(8,128)(2,1)} %collective-permute-done.4), channel_id=1, source_target_pairs={{0,4},{4,8},{8,12},{12,16},{16,20},{20,24},{24,28},{28,0},{1,5},{5... | collective-permute-start | bytes 6291464 | tf_op jit(solution)/shard_map/ppermute | solution.py:20
  201.7 1.6 copy-start.1
  201.7 2.2 copy-start.3
  203.3 1.7 copy-start.5
